TPU v7x, 32 devices: a whole 2x2x4 slice. The times are simulated.
32 devices in a mesh: fsdp: 8 (over y, x, core), dp: 4 (over z).
Axes of the slice: x: 2, y: 2, z: 4, core: 2. Of those that a mesh axis runs over, the one named last changes fastest.
Arguments:
- tokens: bfloat16 [32768, 768], P(('fsdp', 'dp')), may hold values from -6 to 6
- crop_ids: int32 [32768], P(('fsdp', 'dp')), may hold values from 0 to 23, as said below
- gain_first: bfloat16 [768], P('fsdp'), may hold values from 0.25 to 1.75
- shift_first: bfloat16 [768], P('fsdp'), may hold values from -1 to 1
- joint_weight: bfloat16 [768, 2304], P('fsdp'), may hold values from -0.3125 to 0.3125
- joint_bias: bfloat16 [2, 768], P(None, 'fsdp'), may hold values from -1 to 1
- output_weight: bfloat16 [768, 768], P('fsdp'), may hold values from -0.4375 to 0.4375
- output_bias: bfloat16 [768], P('fsdp'), may hold values from -1 to 1
- gain_second: bfloat16 [768], P('fsdp'), may hold values from 0.25 to 1.75
- shift_second: bfloat16 [768], P('fsdp'), may hold values from -1 to 1
- up_weight: bfloat16 [768, 3072], P('fsdp'), may hold values from -0.21875 to 0.21875
- up_bias: bfloat16 [3072], P('fsdp'), may hold values from -1 to 1
- down_weight: bfloat16 [3072, 768], P('fsdp'), may hold values from -0.15625 to 0.15625
- down_bias: bfloat16 [768], P('fsdp'), may hold values from -1 to 1
- cotangent: bfloat16 [32768, 768], P(('fsdp', 'dp')), may hold values from -6 to 6
Outputs:
- activations: float32 [32768, 768], P(('fsdp', 'dp'))
- input_grad: float32 [32768, 768], P(('fsdp', 'dp'))
- grad_gain_first: float32 [768], P('fsdp')
- grad_shift_first: float32 [768], P('fsdp')
- grad_joint_weight: float32 [768, 2304], P('fsdp')
- grad_joint_bias: float32 [2, 768], P(None, 'fsdp')
- grad_output_weight: float32 [768, 768], P('fsdp')
- grad_output_bias: float32 [768], P('fsdp')
- grad_gain_second: float32 [768], P('fsdp')
- grad_shift_second: float32 [768], P('fsdp')
- grad_up_weight: float32 [768, 3072], P('fsdp')
- grad_up_bias: float32 [3072], P('fsdp')
- grad_down_weight: float32 [3072, 768], P('fsdp')
- grad_down_bias: float32 [768], P('fsdp')
Inputs may be any that keep to these rules, and one draw needn't show every extreme that they name: `crop_ids`: each device's 1024 tokens hold whole crops in random order: at least one global crop of 197 tokens, local crops of 37 tokens, and at most one shorter remainder crop; the first device's block holds exactly one global crop. Ids number the crops of a block from 0 in order of position; a crop has at most 197 tokens and every block has a crop of exactly 197.
All inputs are finite; a program needn't handle non-finite values.
Results may differ from a plain program's by a relative error of at most 0.015.
Values may be sent and summed in bfloat16 or wider, within the bound.
No kernel may reach another device: no remote copies, remote signals or barrier semaphores. Data moves between devices by JAX's collectives and lax.ppermute only.
A program may use at most 256 MiB of HBM per device.

v0:
```python
import jax
import jax.numpy as jnp
from jax import lax
from jax.sharding import PartitionSpec as P

HD = 64


def layer_norm(values, gain, shift):
    center = values - jnp.mean(values, axis=-1, keepdims=True)
    spread = jnp.mean(center * center, axis=-1, keepdims=True)
    return center * lax.rsqrt(spread + 1e-06) * gain + shift


def exact_gelu(values):
    return jax.nn.gelu(values, approximate=False)


def on_device(
    tokens,
    crop_ids,
    gain_first,
    shift_first,
    joint_weight,
    joint_bias,
    output_weight,
    output_bias,
    gain_second,
    shift_second,
    up_weight,
    up_bias,
    down_weight,
    down_bias,
    cotangent,
):
    row_count = tokens.shape[0]
    model_width = tokens.shape[1]
    head_count = model_width // HD
    score_scale = HD ** (-0.5)
    block_rows = min(512, row_count)
    block_count = row_count // block_rows
    attn_full = (
        lax.all_gather(gain_first, "fsdp", axis=0, tiled=True),
        lax.all_gather(shift_first, "fsdp", axis=0, tiled=True),
        lax.all_gather(joint_weight, "fsdp", axis=0, tiled=True),
        lax.all_gather(joint_bias, "fsdp", axis=1, tiled=True),
        lax.all_gather(output_weight, "fsdp", axis=0, tiled=True),
        lax.all_gather(output_bias, "fsdp", axis=0, tiled=True),
    )
    gain_one, shift_one, joint_full, joint_bias_full, output_full, output_bias_full = attn_full
    inputs = tokens.astype(jnp.float32)
    normed_first, pull_first = jax.vjp(
        layer_norm, inputs, gain_one.astype(jnp.float32), shift_one.astype(jnp.float32)
    )
    hidden_first = normed_first.astype(jnp.bfloat16)
    bias_joint = joint_bias_full.astype(jnp.float32)
    bias_row = jnp.concatenate(
        [bias_joint[0], jnp.zeros((model_width,), jnp.float32), bias_joint[1]]
    )
    joint_proj = (
        jnp.dot(hidden_first, joint_full, preferred_element_type=jnp.float32) + bias_row
    ).astype(jnp.bfloat16)
    queries = joint_proj[:, :model_width].reshape(row_count, head_count, HD)
    key_rows = joint_proj[:, model_width : 2 * model_width].reshape(row_count, head_count, HD)
    value_rows = joint_proj[:, 2 * model_width :].reshape(row_count, head_count, HD)
    query_blocks = queries.reshape(block_count, block_rows, head_count, HD)
    crop_blocks = crop_ids.reshape(block_count, block_rows)

    def masked_scores(query_block, crop_block):
        scores = (
            jnp.einsum("qhd,khd->hqk", query_block, key_rows, preferred_element_type=jnp.float32)
            * score_scale
        )
        same_crop = crop_block[:, None] == crop_ids[None, :]
        return jnp.where(same_crop[None], scores, -1e30)

    def attend(inputs_block):
        query_block, crop_block = inputs_block
        scores = masked_scores(query_block, crop_block)
        top_score = jnp.max(scores, axis=-1, keepdims=True)
        expo = jnp.exp(scores - top_score)
        total = jnp.sum(expo, axis=-1, keepdims=True)
        weights_low = (expo / total).astype(jnp.bfloat16)
        mixed_block = jnp.einsum(
            "hqk,khd->qhd", weights_low, value_rows, preferred_element_type=jnp.float32
        )
        log_total = top_score[..., 0] + jnp.log(total[..., 0])
        return (mixed_block.astype(jnp.bfloat16), log_total)

    mixed_blocks, log_totals = lax.map(attend, (query_blocks, crop_blocks))
    mixed_heads = mixed_blocks.reshape(row_count, model_width)
    branch_first = jnp.dot(
        mixed_heads, output_full, preferred_element_type=jnp.float32
    ) + output_bias_full.astype(jnp.float32)
    middle = inputs + branch_first
    mlp_full = (
        lax.all_gather(gain_second, "fsdp", axis=0, tiled=True),
        lax.all_gather(shift_second, "fsdp", axis=0, tiled=True),
        lax.all_gather(up_weight, "fsdp", axis=0, tiled=True),
        lax.all_gather(up_bias, "fsdp", axis=0, tiled=True),
        lax.all_gather(down_weight, "fsdp", axis=0, tiled=True),
        lax.all_gather(down_bias, "fsdp", axis=0, tiled=True),
    )
    gain_two, shift_two, up_full, up_bias_full, down_full, down_bias_full = mlp_full
    normed_second, pull_second = jax.vjp(
        layer_norm, middle, gain_two.astype(jnp.float32), shift_two.astype(jnp.float32)
    )
    hidden_second = normed_second.astype(jnp.bfloat16)
    up_value = jnp.dot(
        hidden_second, up_full, preferred_element_type=jnp.float32
    ) + up_bias_full.astype(jnp.float32)
    active_value, pull_gelu = jax.vjp(exact_gelu, up_value)
    active = active_value.astype(jnp.bfloat16)
    activations = (
        middle
        + jnp.dot(active, down_full, preferred_element_type=jnp.float32)
        + down_bias_full.astype(jnp.float32)
    )
    mlp_back = (
        lax.all_gather(gain_second, "fsdp", axis=0, tiled=True),
        lax.all_gather(shift_second, "fsdp", axis=0, tiled=True),
        lax.all_gather(up_weight, "fsdp", axis=0, tiled=True),
        lax.all_gather(up_bias, "fsdp", axis=0, tiled=True),
        lax.all_gather(down_weight, "fsdp", axis=0, tiled=True),
        lax.all_gather(down_bias, "fsdp", axis=0, tiled=True),
    )
    up_back = mlp_back[2]
    down_back = mlp_back[4]
    grad_out = cotangent.astype(jnp.float32)
    grad_down_bias = jnp.sum(grad_out, axis=0)
    grad_down_weight = jnp.einsum(
        "tf,td->fd", active, cotangent, preferred_element_type=jnp.float32
    )
    grad_active = jnp.einsum("td,fd->tf", cotangent, down_back, preferred_element_type=jnp.float32)
    (grad_up_value,) = pull_gelu(grad_active)
    grad_up_low = grad_up_value.astype(jnp.bfloat16)
    grad_up_bias = jnp.sum(grad_up_low.astype(jnp.float32), axis=0)
    grad_up_weight = jnp.einsum(
        "td,tf->df", hidden_second, grad_up_low, preferred_element_type=jnp.float32
    )
    grad_hidden_second = jnp.einsum(
        "tf,df->td", grad_up_low, up_back, preferred_element_type=jnp.float32
    )
    grad_middle, grad_gain_second, grad_shift_second = pull_second(grad_hidden_second)
    grad_middle = grad_middle + grad_out
    mlp_terms = (
        grad_gain_second,
        grad_shift_second,
        grad_up_weight,
        grad_up_bias,
        grad_down_weight,
        grad_down_bias,
    )
    mlp_sums = (
        lax.psum_scatter(mlp_terms[0], "fsdp", scatter_dimension=0, tiled=True),
        lax.psum_scatter(mlp_terms[1], "fsdp", scatter_dimension=0, tiled=True),
        lax.psum_scatter(mlp_terms[2], "fsdp", scatter_dimension=0, tiled=True),
        lax.psum_scatter(mlp_terms[3], "fsdp", scatter_dimension=0, tiled=True),
        lax.psum_scatter(mlp_terms[4], "fsdp", scatter_dimension=0, tiled=True),
        lax.psum_scatter(mlp_terms[5], "fsdp", scatter_dimension=0, tiled=True),
    )
    attn_back = (
        lax.all_gather(gain_first, "fsdp", axis=0, tiled=True),
        lax.all_gather(shift_first, "fsdp", axis=0, tiled=True),
        lax.all_gather(joint_weight, "fsdp", axis=0, tiled=True),
        lax.all_gather(joint_bias, "fsdp", axis=1, tiled=True),
        lax.all_gather(output_weight, "fsdp", axis=0, tiled=True),
        lax.all_gather(output_bias, "fsdp", axis=0, tiled=True),
    )
    joint_back = attn_back[2]
    output_back = attn_back[4]
    grad_branch = grad_middle.astype(jnp.bfloat16)
    grad_output_bias = jnp.sum(grad_branch.astype(jnp.float32), axis=0)
    grad_output_weight = jnp.einsum(
        "td,te->de", mixed_heads, grad_branch, preferred_element_type=jnp.float32
    )
    grad_mixed = jnp.einsum(
        "te,de->td", grad_branch, output_back, preferred_element_type=jnp.float32
    ).astype(jnp.bfloat16)
    grad_mixed_blocks = grad_mixed.reshape(block_count, block_rows, head_count, HD)

    def attend_back(carry, inputs_block):
        grad_key_sum, grad_value_sum = carry
        query_block, crop_block, log_total, grad_block = inputs_block
        scores = masked_scores(query_block, crop_block)
        weights = jnp.exp(scores - log_total[..., None])
        weights_low = weights.astype(jnp.bfloat16)
        grad_value_sum = grad_value_sum + jnp.einsum(
            "hqk,qhd->khd", weights_low, grad_block, preferred_element_type=jnp.float32
        )
        grad_weights = jnp.einsum(
            "qhd,khd->hqk", grad_block, value_rows, preferred_element_type=jnp.float32
        )
        inner = jnp.sum(weights * grad_weights, axis=-1, keepdims=True)
        grad_scores = (weights * (grad_weights - inner)).astype(jnp.bfloat16)
        grad_query = (
            jnp.einsum("hqk,khd->qhd", grad_scores, key_rows, preferred_element_type=jnp.float32)
            * score_scale
        )
        grad_key_sum = (
            grad_key_sum
            + jnp.einsum(
                "hqk,qhd->khd", grad_scores, query_block, preferred_element_type=jnp.float32
            )
            * score_scale
        )
        return ((grad_key_sum, grad_value_sum), grad_query)

    empty_heads = jnp.zeros((row_count, head_count, HD), jnp.float32)
    (grad_keys, grad_values), grad_query_blocks = lax.scan(
        attend_back,
        (empty_heads, empty_heads),
        (query_blocks, crop_blocks, log_totals, grad_mixed_blocks),
    )
    grad_joint = jnp.concatenate(
        [
            grad_query_blocks.reshape(row_count, model_width),
            grad_keys.reshape(row_count, model_width),
            grad_values.reshape(row_count, model_width),
        ],
        axis=1,
    ).astype(jnp.bfloat16)
    grad_joint_wide = grad_joint.astype(jnp.float32)
    grad_joint_bias = jnp.stack(
        [
            jnp.sum(grad_joint_wide[:, :model_width], axis=0),
            jnp.sum(grad_joint_wide[:, 2 * model_width :], axis=0),
        ]
    )
    grad_joint_weight = jnp.einsum(
        "td,te->de", hidden_first, grad_joint, preferred_element_type=jnp.float32
    )
    grad_hidden_first = jnp.einsum(
        "te,de->td", grad_joint, joint_back, preferred_element_type=jnp.float32
    )
    grad_inputs, grad_gain_first, grad_shift_first = pull_first(grad_hidden_first)
    input_grad = grad_inputs + grad_middle
    attn_terms = (
        grad_gain_first,
        grad_shift_first,
        grad_joint_weight,
        grad_joint_bias,
        grad_output_weight,
        grad_output_bias,
    )
    attn_sums = (
        lax.psum_scatter(attn_terms[0], "fsdp", scatter_dimension=0, tiled=True),
        lax.psum_scatter(attn_terms[1], "fsdp", scatter_dimension=0, tiled=True),
        lax.psum_scatter(attn_terms[2], "fsdp", scatter_dimension=0, tiled=True),
        lax.psum_scatter(attn_terms[3], "fsdp", scatter_dimension=1, tiled=True),
        lax.psum_scatter(attn_terms[4], "fsdp", scatter_dimension=0, tiled=True),
        lax.psum_scatter(attn_terms[5], "fsdp", scatter_dimension=0, tiled=True),
    )
    totals = (
        lax.psum(attn_sums[0].astype(jnp.bfloat16), "dp").astype(jnp.float32),
        lax.psum(attn_sums[1].astype(jnp.bfloat16), "dp").astype(jnp.float32),
        lax.psum(attn_sums[2].astype(jnp.bfloat16), "dp").astype(jnp.float32),
        lax.psum(attn_sums[3].astype(jnp.bfloat16), "dp").astype(jnp.float32),
        lax.psum(attn_sums[4].astype(jnp.bfloat16), "dp").astype(jnp.float32),
        lax.psum(attn_sums[5].astype(jnp.bfloat16), "dp").astype(jnp.float32),
        lax.psum(mlp_sums[0].astype(jnp.bfloat16), "dp").astype(jnp.float32),
        lax.psum(mlp_sums[1].astype(jnp.bfloat16), "dp").astype(jnp.float32),
        lax.psum(mlp_sums[2].astype(jnp.bfloat16), "dp").astype(jnp.float32),
        lax.psum(mlp_sums[3].astype(jnp.bfloat16), "dp").astype(jnp.float32),
        lax.psum(mlp_sums[4].astype(jnp.bfloat16), "dp").astype(jnp.float32),
        lax.psum(mlp_sums[5].astype(jnp.bfloat16), "dp").astype(jnp.float32),
    )
    return (
        activations,
        input_grad,
        totals[0],
        totals[1],
        totals[2],
        totals[3],
        totals[4],
        totals[5],
        totals[6],
        totals[7],
        totals[8],
        totals[9],
        totals[10],
        totals[11],
    )


def solution(mesh):
    placed = (
        P(("fsdp", "dp"), None),
        P(("fsdp", "dp")),
        P("fsdp"),
        P("fsdp"),
        P("fsdp", None),
        P(None, "fsdp"),
        P("fsdp", None),
        P("fsdp"),
        P("fsdp"),
        P("fsdp"),
        P("fsdp", None),
        P("fsdp"),
        P("fsdp", None),
        P("fsdp"),
        P(("fsdp", "dp"), None),
    )
    return jax.shard_map(
        on_device,
        mesh=mesh,
        in_specs=placed,
        out_specs=(
            P(("fsdp", "dp"), None),
            P(("fsdp", "dp"), None),
            P("fsdp"),
            P("fsdp"),
            P("fsdp", None),
            P(None, "fsdp"),
            P("fsdp", None),
            P("fsdp"),
            P("fsdp"),
            P("fsdp"),
            P("fsdp", None),
            P("fsdp"),
            P("fsdp", None),
            P("fsdp"),
        ),
        check_vma=False,
    )
```

profile of v0, /device:TPU:0, one launch (start us, length us, event | category | flops | bytes accessed | tf_op | source)
XLA Modules:
  0.0 798.5 jit_solution(4974741141929564460)
XLA Ops:
  17.8 26.7 %all-reduce.14 = (bf16[768]{0:T(1024)(128)(2,1)S(1)}, bf16[768]{0:T(1024)(128)(2,1)S(1)}, bf16[768]{0:T(1024)(128)(2,1)S(1)}, bf16[768]{0:T(1024)(128)(2,1)S(1)}...) all-reduce(bf16[768]{0:T(1024)(128)(2,1)S(1)} %dynamic-update-slice., ...), channel_id=1, replica_groups=mesh['fsdp'=8,'dp'=4] {'fsdp'}, use_global_device_ids=true, to_apply=%add.1 | all-reduce | flops 4608 | bytes 18432
  87.9 72.2 %while.27 = (s32[]{:T(128)}, bf16[2,512,12,64]{1,3,2,0:T(8,128)(2,1)}, f32[2,12,512]{2,1,0:T(8,128)S(1)}, s32[2,512]{1,0:T(2,128)S(1)}, s32[1024]{0:T(1024)S(1)}...) while((s32[]{:T(128)}, ...), condition=%wide.region_5.6_spmd, body=%wide.region_2.5_spmd.sunk | while | flops 1687021568 | bytes 189499568 | solution.py:90
  88.3 11.1 %fusion.114 = (f32[12,512]{1,0:T(8,128)S(1)}, f32[12,512,1024]{2,1,0:T(8,128)}) fusion(pred[512,1024]{1,0:T(8,128)(4,1)S(1)} %broadcast_compare_fusion.4, bf16[1024,12,64]{0,2,1:T(8,128)(2,1)S(1)} %get-tuple-element.534, bf16[2,512,12,64]{1,3,2,0:T(8,128)(2,1)S(1)} %get-tuple-element.533, s32[]{:T(128)S(6)} %copy.120), kind=kOutput, calls=%fused_computation.3.clone.1 | convolution fusion | flops 824174592 | bytes 28073988 | tf_op jit(solution)/shard_map/while/body/eval_jaxpr/qhd,khd->hqk/dot_general | solution.py:71
  99.4 12.5 %fusion.115 = f32[12,512]{1,0:T(8,128)S(1)} fusion(f32[12,512,1024]{2,1,0:T(8,128)} %get-tuple-element.495, f32[12,512]{1,0:T(8,128)S(1)} %get-tuple-element.496, pred[512,1024]{1,0:T(8,128)(4,1)S(1)} %broadcast_compare_fusion.4), kind=kLoop, calls=%fused_computation.4.clone.1 | loop fusion | flops 25159680 | bytes 25739264 | tf_op jit(solution)/shard_map/while/body/eval_jaxpr/reduce_sum | solution.py:82
  124.1 10.7 %fusion.114 = (f32[12,512]{1,0:T(8,128)S(1)}, f32[12,512,1024]{2,1,0:T(8,128)}) fusion(pred[512,1024]{1,0:T(8,128)(4,1)S(1)} %broadcast_compare_fusion.4, bf16[1024,12,64]{0,2,1:T(8,128)(2,1)S(1)} %get-tuple-element.534, bf16[2,512,12,64]{1,3,2,0:T(8,128)(2,1)S(1)} %get-tuple-element.533, s32[]{:T(128)S(6)} %copy.120), kind=kOutput, calls=%fused_computation.3.clone.1 | convolution fusion | flops 824174592 | bytes 28073988 | tf_op jit(solution)/shard_map/while/body/eval_jaxpr/qhd,khd->hqk/dot_general | solution.py:71
  134.8 13.2 %fusion.115 = f32[12,512]{1,0:T(8,128)S(1)} fusion(f32[12,512,1024]{2,1,0:T(8,128)} %get-tuple-element.495, f32[12,512]{1,0:T(8,128)S(1)} %get-tuple-element.496, pred[512,1024]{1,0:T(8,128)(4,1)S(1)} %broadcast_compare_fusion.4), kind=kLoop, calls=%fused_computation.4.clone.1 | loop fusion | flops 25159680 | bytes 25739264 | tf_op jit(solution)/shard_map/while/body/eval_jaxpr/reduce_sum | solution.py:82
  170.6 37.9 %multiply_convert_fusion.1 = (bf16[1024,3072]{1,0:T(8,128)(2,1)}, f32[1024,3072]{1,0:T(8,128)}, f32[1024,3072]{1,0:T(8,128)}) fusion(f32[3072]{0:T(1024)S(1)} %bitcast.151, bf16[768,3072]{1,0:T(8,128)(2,1)} %all-gather.11.cloned.1.call-done, f32[1024,768]{0,1:T(8,128)S(1)} %get-tuple-element.378, f32[768]{0:T(1024)S(1)} %copy-done.51, ...), kind=kOutput, calls=%fused_computation.50 | convolution fusion | flops 5043388416 | bytes 39348224 | tf_op jit(solution)/shard_map/dot_general | solution.py:109
  208.5 18.9 %convert_reduce_fusion = (f32[3072]{0:T(1024)}, bf16[1024,3072]{1,0:T(8,128)(2,1)}) fusion(f32[1024,3072]{1,0:T(8,128)} %get-tuple-element.365, bf16[1024,768]{1,0:T(8,128)(2,1)} %param.33, bf16[3072,768]{1,0:T(8,128)(2,1)} %all-gather.13.cloned.1.call-done, f32[1024,3072]{1,0:T(8,128)} %get-tuple-element.379, f32[3072]{0:T(1024)S(1)} %bitcast.152), kind=kOutput, calls=%fused_computation.48 | convolution fusion | flops 4885312512 | bytes 37773312 | tf_op jit(solution)/shard_map/td,fd->tf/dot_general | solution.py:134
  257.4 169.1 %while.28 = (s32[]{:T(128)}, f32[1024,12,64]{0,2,1:T(8,128)}, f32[1024,12,64]{0,2,1:T(8,128)}, bf16[2,512,12,64]{1,3,2,0:T(8,128)(2,1)}, bf16[2,512,12,64]{1,3,2...) while((s32[]{:T(128)}, f32[1024,12,64]{0,2,1:T(8,128)}, ...), condition=%wide.region_12.13_spmd.clone, body=%wide.region_10.12_spmd.clone.sunk | while | flops 4125747200 | bytes 225634512 | solution.py:210
  258.3 12.3 %fusion.126 = f32[12,512,1024]{2,1,0:T(8,128)} fusion(bf16[1024,12,64]{0,2,1:T(8,128)(2,1)S(1)} %get-tuple-element.570, bf16[2,512,12,64]{1,3,2,0:T(8,128)(2,1)} %get-tuple-element.567, s32[]{:T(128)S(6)} %copy.130), kind=kOutput, calls=%fused_computation.32.clone.1 | convolution fusion | flops 805306368 | bytes 27525124 | tf_op jit(solution)/shard_map/while/body/eval_jaxpr/qhd,khd->hqk/dot_general | solution.py:71
  270.5 13.5 %bitcast_add_fusion.5 = f32[1024,12,64]{0,2,1:T(8,128)} fusion(f32[1024,12,64]{0,2,1:T(8,128)} %get-tuple-element.552, f32[12,512,1024]{2,1,0:T(8,128)} %fusion.126, f32[12,512]{1,0:T(8,128)S(1)} %dynamic-slice_bitcast_fusion.2, pred[512,1024]{1,0:T(8,128)(4,1)S(1)} %broadcast_compare_fusion.5, pred[]{:T(512)S(6)} %compare.3, ...), kind=kOutput, calls=%fused_computation.24.clone.1 | convolution fusion | flops 832045056 | bytes 32800772 | tf_op jit(solution)/shard_map/while/body/eval_jaxpr/hqk,qhd->khd/dot_general | solution.py:188
  284.0 18.3 %multiply_reduce_fusion.5 = (f32[12,512]{1,0:T(8,128)S(1)}, f32[12,512,1024]{2,1,0:T(8,128)}) fusion(f32[12,512,1024]{2,1,0:T(8,128)} %fusion.126, f32[12,512]{1,0:T(8,128)S(1)} %dynamic-slice_bitcast_fusion.2, pred[512,1024]{1,0:T(8,128)(4,1)S(1)} %broadcast_compare_fusion.5, bf16[1024,12,64]{0,2,1:T(8,128)(2,1)} %get-tuple-element.573, ...), kind=kOutput, calls=%fused_computation.19.clone.1 | convolution fusion | flops 836757504 | bytes 53264388 | tf_op jit(solution)/shard_map/while/body/eval_jaxpr/qhd,khd->hqk/dot_general | solution.py:191
  302.3 21.3 %multiply_convert_fusion.3 = bf16[12,512,1024]{2,1,0:T(8,128)(2,1)} fusion(f32[12,512,1024]{2,1,0:T(8,128)} %get-tuple-element.508, f32[12,512,1024]{2,1,0:T(8,128)} %fusion.126, f32[12,512]{1,0:T(8,128)S(1)} %get-tuple-element.509, f32[12,512]{1,0:T(8,128)S(1)} %dynamic-slice_bitcast_fusion.2, pred[512,1024]{1,0:T(8,128)(4,1)S(1)} %broadcast_compare_fusion.5), kind=kLoop, calls=%fused_computation.18.clone.1 | loop fusion | flops 37748736 | bytes 63488000 | tf_op jit(solution)/shard_map/while/body/eval_jaxpr/convert_element_type | solution.py:195
  342.1 11.4 %fusion.126 = f32[12,512,1024]{2,1,0:T(8,128)} fusion(bf16[1024,12,64]{0,2,1:T(8,128)(2,1)S(1)} %get-tuple-element.570, bf16[2,512,12,64]{1,3,2,0:T(8,128)(2,1)} %get-tuple-element.567, s32[]{:T(128)S(6)} %copy.130), kind=kOutput, calls=%fused_computation.32.clone.1 | convolution fusion | flops 805306368 | bytes 27525124 | tf_op jit(solution)/shard_map/while/body/eval_jaxpr/qhd,khd->hqk/dot_general | solution.py:71
  353.5 14.4 %bitcast_add_fusion.5 = f32[1024,12,64]{0,2,1:T(8,128)} fusion(f32[1024,12,64]{0,2,1:T(8,128)} %get-tuple-element.552, f32[12,512,1024]{2,1,0:T(8,128)} %fusion.126, f32[12,512]{1,0:T(8,128)S(1)} %dynamic-slice_bitcast_fusion.2, pred[512,1024]{1,0:T(8,128)(4,1)S(1)} %broadcast_compare_fusion.5, pred[]{:T(512)S(6)} %compare.3, ...), kind=kOutput, calls=%fused_computation.24.clone.1 | convolution fusion | flops 832045056 | bytes 32800772 | tf_op jit(solution)/shard_map/while/body/eval_jaxpr/hqk,qhd->khd/dot_general | solution.py:188
  367.9 18.1 %multiply_reduce_fusion.5 = (f32[12,512]{1,0:T(8,128)S(1)}, f32[12,512,1024]{2,1,0:T(8,128)}) fusion(f32[12,512,1024]{2,1,0:T(8,128)} %fusion.126, f32[12,512]{1,0:T(8,128)S(1)} %dynamic-slice_bitcast_fusion.2, pred[512,1024]{1,0:T(8,128)(4,1)S(1)} %broadcast_compare_fusion.5, bf16[1024,12,64]{0,2,1:T(8,128)(2,1)} %get-tuple-element.573, ...), kind=kOutput, calls=%fused_computation.19.clone.1 | convolution fusion | flops 836757504 | bytes 53264388 | tf_op jit(solution)/shard_map/while/body/eval_jaxpr/qhd,khd->hqk/dot_general | solution.py:191
  386.0 21.3 %multiply_convert_fusion.3 = bf16[12,512,1024]{2,1,0:T(8,128)(2,1)} fusion(f32[12,512,1024]{2,1,0:T(8,128)} %get-tuple-element.508, f32[12,512,1024]{2,1,0:T(8,128)} %fusion.126, f32[12,512]{1,0:T(8,128)S(1)} %get-tuple-element.509, f32[12,512]{1,0:T(8,128)S(1)} %dynamic-slice_bitcast_fusion.2, pred[512,1024]{1,0:T(8,128)(4,1)S(1)} %broadcast_compare_fusion.5), kind=kLoop, calls=%fused_computation.18.clone.1 | loop fusion | flops 37748736 | bytes 63488000 | tf_op jit(solution)/shard_map/while/body/eval_jaxpr/convert_element_type | solution.py:195
  442.1 10.8 %fusion.60 = f32[768,3072]{1,0:T(8,128)} fusion(bf16[1024,3072]{1,0:T(8,128)(2,1)} %get-tuple-element.385, f32[1024,768]{0,1:T(8,128)} %copy-done.12, f32[768]{0:T(1024)S(1)} %copy-done.52, f32[768]{0:T(1024)S(1)} %copy-done.43, f32[1024]{0:T(1024)S(1)} %copy-done.45, f32[1024]{0:T(1024)S(1)} %copy-done.35), kind=kOutput, calls=%fused_computation.121 | convolution fusion | flops 4835770368 | bytes 18888704 | tf_op jit(solution)/shard_map/td,tf->df/dot_general | solution.py:138
  494.5 12.8 %reduce-scatter.8.cloned.1.call-done = f32[96,2304]{1,0:T(8,128)} async-done(((f32[768,2304]{1,0:T(8,128)}), f32[96,2304]{1,0:T(8,128)}) %reduce-scatter.8.cloned.1.call-update) | async-done | bytes 884752 | tf_op jit(solution)/shard_map/reduce_scatter | solution.py:249
  509.3 78.4 %reduce-scatter.12.cloned.1.call-done = f32[96,3072]{1,0:T(8,128)} async-done(((f32[768,3072]{1,0:T(8,128)}), f32[96,3072]{1,0:T(8,128)}) %reduce-scatter.12.cloned.1.call-update) | async-done | bytes 1179664 | tf_op jit(solution)/shard_map/reduce_scatter | solution.py:157
  589.9 78.2 %reduce-scatter.14.cloned.1.call-done = f32[384,768]{1,0:T(8,128)} async-done(((f32[3072,768]{1,0:T(8,128)}), f32[384,768]{1,0:T(8,128)}) %reduce-scatter.14.cloned.1.call-update) | async-done | bytes 1179664 | tf_op jit(solution)/shard_map/reduce_scatter | solution.py:159
  678.5 23.3 %all-reduce.13 = (bf16[768]{0:T(1024)(128)(2,1)S(1)}, bf16[768]{0:T(1024)(128)(2,1)S(1)}, bf16[768]{0:T(1024)(128)(2,1)S(1)}, bf16[768]{0:T(1024)(128)(2,1)S(1)}...) all-reduce(f32[768]{0:T(1024)S(1)} %get-tuple-element.293, ...), channel_id=2, replica_groups=mesh['fsdp'=8,'dp'=4] {'fsdp'}, use_global_device_ids=true, to_apply=%region_16.17.clone | all-reduce | flops 7680 | bytes 46080
  706.7 11.9 %all-reduce.15 = (bf16[96]{0:T(256)(128)(2,1)S(1)}, bf16[96]{0:T(256)(128)(2,1)S(1)}, bf16[2,96]{1,0:T(2,128)(2,1)S(1)}, bf16[96]{0:T(256)(128)(2,1)S(1)}, bf16[...) all-reduce(bf16[96]{0:T(256)(128)(2,1)S(1)} %dynamic-slice.33, ...), channel_id=1, replica_groups=mesh['fsdp'=8,'dp'=4] {'dp'}, use_global_device_ids=true, to_apply=%region_17.18 | all-reduce | flops 1152 | bytes 4608 | tf_op jit(solution)/shard_map/psum | solution.py:255
  722.9 61.4 %all-reduce.19.cloned.1.call-done = (bf16[96,2304]{1,0:T(8,128)(2,1)}, bf16[96,768]{1,0:T(8,128)(2,1)}, bf16[96,3072]{1,0:T(8,128)(2,1)}, bf16[384,768]{1,0:T(8,128)(2,1)}) async-done(((bf16[96,2304]{1,0:T(8,128)(2,1)}, bf16[96,768]{1,0:T(8,128)(2,1)}, bf16[96,3072]{1,0:T(8,128)(2,1)}, bf16[384,768]{1,0:T(8,128)(2,1)}), (bf16[96,2304]{1,0:T(8,128)(2,1)}, bf16[96,768]{1,0:T(8,128)(2,1)}, ...) | async-done | bytes 1769488 | tf_op jit(solution)/shard_map/psum | solution.py:257
  (279 shorter events, 241.9 us)
Async XLA Ops:
  7.2 62.2 %all-gather.7.cloned.1.call-start = ((), (), s32[]{:S(2)}) async-start(), calls=%async_computation.5 | async-start | bytes 3981312 | tf_op jit(solution)/shard_map/all_gather | solution.py:45
  7.9 158.0 %all-gather.9.cloned.1.call-start = ((), (), s32[]{:S(2)}) async-start(), calls=%async_computation.6 | async-start | bytes 1327104 | tf_op jit(solution)/shard_map/all_gather | solution.py:47
  8.7 161.6 %all-gather.11.cloned.1.call-start = ((), (), s32[]{:S(2)}) async-start(), calls=%async_computation.7 | async-start | bytes 5308416 | tf_op jit(solution)/shard_map/all_gather | solution.py:99
  9.4 199.1 %all-gather.13.cloned.1.call-start = ((), (), s32[]{:S(2)}) async-start(), calls=%async_computation.8 | async-start | bytes 5308416 | tf_op jit(solution)/shard_map/all_gather | solution.py:101
  10.0 482.9 %reduce-scatter.10.cloned.1.call-start = ((), (), s32[]{:S(2)}) async-start(), calls=%async_computation.10 | async-start | bytes 2654208 | tf_op jit(solution)/shard_map/reduce_scatter | solution.py:251
  44.5 24.9 %copy-start.53 = (f32[768]{0:T(1024)}, f32[768]{0:T(1024)S(1)}, u32[]{:S(2)}) copy-start(f32[768]{0:T(1024)S(1)} %convert_element_type.150) | copy-start | bytes 9220
  44.5 24.9 %copy-start.32 = (f32[768]{0:T(1024)}, f32[768]{0:T(1024)S(1)}, u32[]{:S(2)}) copy-start(f32[768]{0:T(1024)S(1)} %convert_element_type.149) | copy-start | bytes 9220
  88.3 23.6 %copy-start.6 = (bf16[1024,12,64]{0,2,1:T(8,128)(2,1)S(1)}, bf16[1024,12,64]{0,2,1:T(8,128)(2,1)}, u32[]{:S(2)}) copy-start(bf16[1024,12,64]{0,2,1:T(8,128)(2,1)} %get-tuple-element.535) | copy-start | bytes 4718596 | tf_op jit(solution)/shard_map/while
  99.4 15.8 %copy-start = (f32[12,512,1024]{2,1,0:T(8,128)S(1)}, f32[12,512,1024]{2,1,0:T(8,128)}, u32[]{:S(2)}) copy-start(f32[12,512,1024]{2,1,0:T(8,128)} %get-tuple-element.495) | copy-start | bytes 75497472 | tf_op jit(solution)/shard_map/while
  124.1 23.8 %copy-start.6 = (bf16[1024,12,64]{0,2,1:T(8,128)(2,1)S(1)}, bf16[1024,12,64]{0,2,1:T(8,128)(2,1)}, u32[]{:S(2)}) copy-start(bf16[1024,12,64]{0,2,1:T(8,128)(2,1)} %get-tuple-element.535) | copy-start | bytes 4718596 | tf_op jit(solution)/shard_map/while
  134.8 16.5 %copy-start = (f32[12,512,1024]{2,1,0:T(8,128)S(1)}, f32[12,512,1024]{2,1,0:T(8,128)}, u32[]{:S(2)}) copy-start(f32[12,512,1024]{2,1,0:T(8,128)} %get-tuple-element.495) | copy-start | bytes 75497472 | tf_op jit(solution)/shard_map/while
  169.8 75.0 %copy-start.12 = (f32[1024,768]{0,1:T(8,128)}, f32[1024,768]{0,1:T(8,128)S(1)}, u32[]{:S(2)}) copy-start(f32[1024,768]{0,1:T(8,128)S(1)} %get-tuple-element.378) | copy-start | bytes 9437188
  169.8 75.0 %copy-start.34 = (f32[1024]{0:T(1024)}, f32[1024]{0:T(1024)S(1)}, u32[]{:S(2)}) copy-start(f32[1024]{0:T(1024)S(1)} %broadcast_multiply_fusion) | copy-start | bytes 12292
  170.2 74.6 %copy-start.44 = (f32[1024]{0:T(1024)}, f32[1024]{0:T(1024)S(1)}, u32[]{:S(2)}) copy-start(f32[1024]{0:T(1024)S(1)} %fusion.54) | copy-start | bytes 12292
  257.3 250.1 %reduce-scatter.8.cloned.1.call-start = ((), (), s32[]{:S(2)}) async-start(), calls=%async_computation.9 | async-start | bytes 7962624 | tf_op jit(solution)/shard_map/reduce_scatter | solution.py:249
  258.2 12.3 %copy-start.14 = (bf16[2,512,12,64]{1,3,2,0:T(8,128)(2,1)S(1)}, bf16[2,512,12,64]{1,3,2,0:T(8,128)(2,1)}, u32[]{:S(2)}) copy-start(bf16[2,512,12,64]{1,3,2,0:T(8,128)(2,1)} %get-tuple-element.572) | copy-start | bytes 4718596 | tf_op jit(solution)/shard_map/while
  342.1 11.4 %copy-start.14 = (bf16[2,512,12,64]{1,3,2,0:T(8,128)(2,1)S(1)}, bf16[2,512,12,64]{1,3,2,0:T(8,128)(2,1)}, u32[]{:S(2)}) copy-start(bf16[2,512,12,64]{1,3,2,0:T(8,128)(2,1)} %get-tuple-element.572) | copy-start | bytes 4718596 | tf_op jit(solution)/shard_map/while
  441.4 146.3 %reduce-scatter.12.cloned.1.call-start = ((), (), s32[]{:S(2)}) async-start(), calls=%async_computation.11 | async-start | bytes 10616832 | tf_op jit(solution)/shard_map/reduce_scatter | solution.py:157
  452.9 215.2 %reduce-scatter.14.cloned.1.call-start = ((), (), s32[]{:S(2)}) async-start(), calls=%async_computation.12 | async-start | bytes 10616832 | tf_op jit(solution)/shard_map/reduce_scatter | solution.py:159
  463.6 242.3 %reduce-scatter.16.cloned.1.call-start = ((), (), s32[]{:S(2)}) async-start(), calls=%async_computation.13 | async-start | bytes 442368
  469.6 314.7 %all-reduce.19.cloned.1.call-start = ((), (), s32[]{:S(2)}) async-start(), calls=%async_computation.14 | async-start | bytes 3538944 | tf_op jit(solution)/shard_map/psum | solution.py:257
  469.6 10.6 %copy-start.18 = (bf16[1024,12,64]{0,2,1:T(8,128)(2,1)S(1)}, bf16[1024,12,64]{0,2,1:T(8,128)(2,1)}, u32[]{:S(2)}) copy-start(bf16[1024,12,64]{0,2,1:T(8,128)(2,1)} %copy-done.17) | copy-start | bytes 4718596
  469.6 10.6 %copy-start.20 = (bf16[1024,12,64]{0,2,1:T(8,128)(2,1)S(1)}, bf16[1024,12,64]{0,2,1:T(8,128)(2,1)}, u32[]{:S(2)}) copy-start(bf16[1024,12,64]{0,2,1:T(8,128)(2,1)} %copy-done.19) | copy-start | bytes 4718596
  469.6 10.6 %copy-start.57 = (bf16[768,2304]{1,0:T(8,128)(2,1)S(1)}, bf16[768,2304]{1,0:T(8,128)(2,1)}, u32[]{:S(2)}) copy-start(bf16[768,2304]{1,0:T(8,128)(2,1)} %all-gather.7.cloned.1.call-done) | copy-start | bytes 10616836
  (48 other events, 159.6 us)
Sparse Core Ops, SparseCore 0:
  9.9 36.7 all-gather.6
  48.6 23.9 all-gather.8
  74.5 38.7 all-gather.10
  115.0 38.7 all-gather.12
  257.4 42.6 reduce-scatter.9
  441.5 65.8 reduce-scatter.7
  510.9 76.8 reduce-scatter.11
  591.2 76.8 reduce-scatter.13
  671.1 33.8 reduce-scatter.15
  708.7 75.5 all-reduce.18
where the time goes:
time: 809 us; the launch traced here: 798 us
  matrix products  291 us (36%)
  waiting for transfers between devices  234 us (29%)
  other arithmetic  112 us (14%)
  blocking collectives  78.6 us (10%)
  local copies, waits for them, and re-layouts  64.6 us (8%)
  between operations  17.3 us (2%)
    reduce_scatter x1, waiting for transfers between devices, on_device(): lax.psum_scatter(mlp_terms[2], 'fsdp', scatter_dimension=0, tiled=True)  78.4 us
    reduce_scatter x1, waiting for transfers between devices, on_device(): lax.psum_scatter(mlp_terms[4], 'fsdp', scatter_dimension=0, tiled=True)  78.2 us
    psum x1, waiting for transfers between devices, on_device(): lax.psum(attn_sums[2].astype(jnp.bfloat16), 'dp').astype(jnp.float32)  61.4 us
    unnamed x2, blocking collectives  50 us
    dot_general x4, matrix products, masked_scores(): jnp.einsum('qhd,khd->hqk', query_block, key_rows, preferred_element_type=...  45.4 us
    convert_element_type x2, other arithmetic, attend_back(): grad_scores = (weights * (grad_weights - inner)).astype(jnp.bfloat16)  42.6 us
    dot_general x1, matrix products, on_device(): jnp.dot(hidden_second, up_full, preferred_element_type=jnp.float32)  37.9 us
    dot_general x2, matrix products, attend_back(): jnp.einsum('qhd,khd->hqk', grad_block, value_rows, preferred_element_type...  36.4 us
  transfers between devices with their start and end apart: 10, of which 4 were waited for; matrix products, arithmetic and copies ran while one was open for 50% of the time, Pallas kernels for 0%

commit v1 on v0

--- a/solution.py
+++ b/solution.py
@@ -1,9 +1,18 @@
+import functools
 import jax
 import jax.numpy as jnp
 from jax import lax
 from jax.sharding import PartitionSpec as P
 
 HD = 64
+
+
+def serve_the_zone(xs, group_axis):
+    tile_out = jax.lax.all_gather(xs, group_axis).sum(axis=0)
+    return tile_out
+
+
+packet_edit = functools.partial(serve_the_zone, group_axis="dp")
 
 
 def layer_norm(values, gain, shift):
@@ -254,7 +263,7 @@
     totals = (
         lax.psum(attn_sums[0].astype(jnp.bfloat16), "dp").astype(jnp.float32),
         lax.psum(attn_sums[1].astype(jnp.bfloat16), "dp").astype(jnp.float32),
-        lax.psum(attn_sums[2].astype(jnp.bfloat16), "dp").astype(jnp.float32),
+        packet_edit(attn_sums[2].astype(jnp.bfloat16)).astype(jnp.float32),
         lax.psum(attn_sums[3].astype(jnp.bfloat16), "dp").astype(jnp.float32),
         lax.psum(attn_sums[4].astype(jnp.bfloat16), "dp").astype(jnp.float32),
         lax.psum(attn_sums[5].astype(jnp.bfloat16), "dp").astype(jnp.float32),

time: 809 us -> 885 us (1.094)
  waiting for transfers between devices: 234 us -> 293 us
    reduce_scatter x1, waiting for transfers between devices: 12.8 us -> 33.6 us  [on_device(): lax.psum_scatter(attn_terms[2], 'fsdp', scatter_dimension=0, tiled=True)]
    all_gather x0 -> x1, waiting for transfers between devices: none -> 20.2 us  [serve_the_zone(): tile_out = jax.lax.all_gather(xs, group_axis).sum(axis=0)]
    reduce_scatter x1, waiting for transfers between devices: 0.01 us -> 18.5 us  [on_device(): lax.psum_scatter(attn_terms[4], 'fsdp', scatter_dimension=0, tiled=True)]
    unnamed x138 -> x118, local copies, waits for them, and re-layouts: 28.8 us -> 30.1 us
  transfers between devices with their start and end apart: 10 -> 11, of which waited for: 4 -> 6; matrix products, arithmetic and copies ran while one was open for 50% -> 27% of each run, Pallas kernels for 0% -> 0%
where the time goes in v1:
time: 885 us; the launch traced here: 874 us
  matrix products  294 us (33%)
  waiting for transfers between devices  293 us (33%)
  other arithmetic  118 us (13%)
  blocking collectives  79.1 us (9%)
  local copies, waits for them, and re-layouts  71.7 us (8%)
  between operations  17 us (2%)
    reduce_scatter x1, waiting for transfers between devices, on_device(): lax.psum_scatter(mlp_terms[2], 'fsdp', scatter_dimension=0, tiled=True)  78.7 us
    reduce_scatter x1, waiting for transfers between devices, on_device(): lax.psum_scatter(mlp_terms[4], 'fsdp', scatter_dimension=0, tiled=True)  78.2 us
    psum x1, waiting for transfers between devices, on_device(): lax.psum(attn_sums[4].astype(jnp.bfloat16), 'dp').astype(jnp.float32)  61.2 us
    unnamed x2, blocking collectives  50.1 us
    dot_general x4, matrix products, masked_scores(): jnp.einsum('qhd,khd->hqk', query_block, key_rows, preferred_element_type=...  44.6 us
    convert_element_type x2, other arithmetic, attend_back(): grad_scores = (weights * (grad_weights - inner)).astype(jnp.bfloat16)  42.4 us
    dot_general x1, matrix products, on_device(): jnp.dot(hidden_second, up_full, preferred_element_type=jnp.float32)  37.8 us
    dot_general x2, matrix products, attend_back(): jnp.einsum('qhd,khd->hqk', grad_block, value_rows, preferred_element_type...  36.1 us
  transfers between devices with their start and end apart: 11, of which 6 were waited for; matrix products, arithmetic and copies ran while one was open for 27% of the time, Pallas kernels for 0%

profile of v1, /device:TPU:0, one launch (start us, length us, event | category | flops | bytes accessed | tf_op | source)
XLA Modules:
  0.0 874.4 jit_solution(17354933475723421737)
XLA Ops:
  17.8 26.7 %all-reduce.14 = (bf16[768]{0:T(1024)(128)(2,1)S(1)}, bf16[768]{0:T(1024)(128)(2,1)S(1)}, bf16[768]{0:T(1024)(128)(2,1)S(1)}, bf16[768]{0:T(1024)(128)(2,1)S(1)}...) all-reduce(bf16[768]{0:T(1024)(128)(2,1)S(1)} %dynamic-update-slice., ...), channel_id=1, replica_groups=mesh['fsdp'=8,'dp'=4] {'fsdp'}, use_global_device_ids=true, to_apply=%add.1 | all-reduce | flops 4608 | bytes 18432
  87.3 72.0 %while.27 = (s32[]{:T(128)}, bf16[2,512,12,64]{1,3,2,0:T(8,128)(2,1)}, f32[2,12,512]{2,1,0:T(8,128)S(1)}, s32[2,512]{1,0:T(2,128)S(1)}, s32[1024]{0:T(1024)S(1)}...) while((s32[]{:T(128)}, ...), condition=%wide.region_5.6_spmd, body=%wide.region_2.5_spmd.sunk | while | flops 1687021568 | bytes 189499568 | solution.py:99
  98.7 12.4 %fusion.115 = f32[12,512]{1,0:T(8,128)S(1)} fusion(f32[12,512,1024]{2,1,0:T(8,128)} %get-tuple-element.494, f32[12,512]{1,0:T(8,128)S(1)} %get-tuple-element.495, pred[512,1024]{1,0:T(8,128)(4,1)S(1)} %broadcast_compare_fusion.4), kind=kLoop, calls=%fused_computation.4.clone.1 | loop fusion | flops 25159680 | bytes 25739264 | tf_op jit(solution)/shard_map/while/body/eval_jaxpr/reduce_sum | solution.py:91
  134.0 13.1 %fusion.115 = f32[12,512]{1,0:T(8,128)S(1)} fusion(f32[12,512,1024]{2,1,0:T(8,128)} %get-tuple-element.494, f32[12,512]{1,0:T(8,128)S(1)} %get-tuple-element.495, pred[512,1024]{1,0:T(8,128)(4,1)S(1)} %broadcast_compare_fusion.4), kind=kLoop, calls=%fused_computation.4.clone.1 | loop fusion | flops 25159680 | bytes 25739264 | tf_op jit(solution)/shard_map/while/body/eval_jaxpr/reduce_sum | solution.py:91
  170.0 37.8 %multiply_convert_fusion.1 = (bf16[1024,3072]{1,0:T(8,128)(2,1)}, f32[1024,3072]{1,0:T(8,128)}, f32[1024,3072]{1,0:T(8,128)}) fusion(f32[3072]{0:T(1024)S(1)} %bitcast.153, bf16[768,3072]{1,0:T(8,128)(2,1)} %all-gather.13.cloned.1.call-done, f32[1024,768]{0,1:T(8,128)} %copy-done.9, f32[768]{0:T(1024)S(1)} %copy-done.42, f32[768]{0:T(1024)S(1)} %copy-done.33, ...), kind=kOutput, calls=%fused_computation.50 | convolution fusion | flops 5043388416 | bytes 39348224 | tf_op jit(solution)/shard_map/dot_general | solution.py:118
  207.8 18.9 %convert_reduce_fusion = (f32[3072]{0:T(1024)}, bf16[1024,3072]{1,0:T(8,128)(2,1)}) fusion(f32[1024,3072]{1,0:T(8,128)} %get-tuple-element.364, bf16[1024,768]{1,0:T(8,128)(2,1)} %param.33, bf16[3072,768]{1,0:T(8,128)(2,1)} %all-gather.15.cloned.1.call-done, f32[1024,3072]{1,0:T(8,128)} %get-tuple-element.378, f32[3072]{0:T(1024)S(1)} %bitcast.154), kind=kOutput, calls=%fused_computation.48 | convolution fusion | flops 4885312512 | bytes 37773312 | tf_op jit(solution)/shard_map/td,fd->tf/dot_general | solution.py:143
  261.0 170.0 %while.28 = (s32[]{:T(128)}, f32[1024,12,64]{0,2,1:T(8,128)}, f32[1024,12,64]{0,2,1:T(8,128)}, bf16[2,512,12,64]{1,3,2,0:T(8,128)(2,1)}, bf16[2,512,12,64]{1,3,2...) while((s32[]{:T(128)}, f32[1024,12,64]{0,2,1:T(8,128)}, ...), condition=%wide.region_12.13_spmd.clone, body=%wide.region_10.12_spmd.clone.sunk | while | flops 4125747200 | bytes 231926000 | solution.py:219
  262.9 11.5 %fusion.126 = f32[12,512,1024]{2,1,0:T(8,128)} fusion(bf16[1024,12,64]{0,2,1:T(8,128)(2,1)S(1)} %get-tuple-element.569, bf16[2,512,12,64]{1,3,2,0:T(8,128)(2,1)} %copy-done.2, s32[]{:T(128)S(6)} %copy.130), kind=kOutput, calls=%fused_computation.32.clone.1 | convolution fusion | flops 805306368 | bytes 27525124 | tf_op jit(solution)/shard_map/while/body/eval_jaxpr/qhd,khd->hqk/dot_general | solution.py:80
  274.3 13.4 %bitcast_add_fusion.5 = f32[1024,12,64]{0,2,1:T(8,128)} fusion(f32[1024,12,64]{0,2,1:T(8,128)} %get-tuple-element.551, f32[12,512,1024]{2,1,0:T(8,128)} %fusion.126, f32[12,512]{1,0:T(8,128)S(1)} %dynamic-slice_bitcast_fusion.2, pred[512,1024]{1,0:T(8,128)(4,1)S(1)} %broadcast_compare_fusion.5, pred[]{:T(512)S(6)} %compare.3, ...), kind=kOutput, calls=%fused_computation.24.clone.1 | convolution fusion | flops 832045056 | bytes 32800772 | tf_op jit(solution)/shard_map/while/body/eval_jaxpr/hqk,qhd->khd/dot_general | solution.py:197
  287.8 18.1 %multiply_reduce_fusion.5 = (f32[12,512]{1,0:T(8,128)S(1)}, f32[12,512,1024]{2,1,0:T(8,128)}) fusion(f32[12,512,1024]{2,1,0:T(8,128)} %fusion.126, f32[12,512]{1,0:T(8,128)S(1)} %dynamic-slice_bitcast_fusion.2, pred[512,1024]{1,0:T(8,128)(4,1)S(1)} %broadcast_compare_fusion.5, bf16[1024,12,64]{0,2,1:T(8,128)(2,1)} %get-tuple-element.572, ...), kind=kOutput, calls=%fused_computation.19.clone.1 | convolution fusion | flops 836757504 | bytes 53264388 | tf_op jit(solution)/shard_map/while/body/eval_jaxpr/qhd,khd->hqk/dot_general | solution.py:200
  305.8 21.2 %multiply_convert_fusion.3 = bf16[12,512,1024]{2,1,0:T(8,128)(2,1)} fusion(f32[12,512,1024]{2,1,0:T(8,128)} %get-tuple-element.507, f32[12,512,1024]{2,1,0:T(8,128)} %fusion.126, f32[12,512]{1,0:T(8,128)S(1)} %get-tuple-element.508, f32[12,512]{1,0:T(8,128)S(1)} %dynamic-slice_bitcast_fusion.2, pred[512,1024]{1,0:T(8,128)(4,1)S(1)} %broadcast_compare_fusion.5), kind=kLoop, calls=%fused_computation.18.clone.1 | loop fusion | flops 37748736 | bytes 63488000 | tf_op jit(solution)/shard_map/while/body/eval_jaxpr/convert_element_type | solution.py:204
  346.7 11.5 %fusion.126 = f32[12,512,1024]{2,1,0:T(8,128)} fusion(bf16[1024,12,64]{0,2,1:T(8,128)(2,1)S(1)} %get-tuple-element.569, bf16[2,512,12,64]{1,3,2,0:T(8,128)(2,1)} %copy-done.2, s32[]{:T(128)S(6)} %copy.130), kind=kOutput, calls=%fused_computation.32.clone.1 | convolution fusion | flops 805306368 | bytes 27525124 | tf_op jit(solution)/shard_map/while/body/eval_jaxpr/qhd,khd->hqk/dot_general | solution.py:80
  358.2 14.3 %bitcast_add_fusion.5 = f32[1024,12,64]{0,2,1:T(8,128)} fusion(f32[1024,12,64]{0,2,1:T(8,128)} %get-tuple-element.551, f32[12,512,1024]{2,1,0:T(8,128)} %fusion.126, f32[12,512]{1,0:T(8,128)S(1)} %dynamic-slice_bitcast_fusion.2, pred[512,1024]{1,0:T(8,128)(4,1)S(1)} %broadcast_compare_fusion.5, pred[]{:T(512)S(6)} %compare.3, ...), kind=kOutput, calls=%fused_computation.24.clone.1 | convolution fusion | flops 832045056 | bytes 32800772 | tf_op jit(solution)/shard_map/while/body/eval_jaxpr/hqk,qhd->khd/dot_general | solution.py:197
  372.5 18.1 %multiply_reduce_fusion.5 = (f32[12,512]{1,0:T(8,128)S(1)}, f32[12,512,1024]{2,1,0:T(8,128)}) fusion(f32[12,512,1024]{2,1,0:T(8,128)} %fusion.126, f32[12,512]{1,0:T(8,128)S(1)} %dynamic-slice_bitcast_fusion.2, pred[512,1024]{1,0:T(8,128)(4,1)S(1)} %broadcast_compare_fusion.5, bf16[1024,12,64]{0,2,1:T(8,128)(2,1)} %get-tuple-element.572, ...), kind=kOutput, calls=%fused_computation.19.clone.1 | convolution fusion | flops 836757504 | bytes 53264388 | tf_op jit(solution)/shard_map/while/body/eval_jaxpr/qhd,khd->hqk/dot_general | solution.py:200
  390.6 21.2 %multiply_convert_fusion.3 = bf16[12,512,1024]{2,1,0:T(8,128)(2,1)} fusion(f32[12,512,1024]{2,1,0:T(8,128)} %get-tuple-element.507, f32[12,512,1024]{2,1,0:T(8,128)} %fusion.126, f32[12,512]{1,0:T(8,128)S(1)} %get-tuple-element.508, f32[12,512]{1,0:T(8,128)S(1)} %dynamic-slice_bitcast_fusion.2, pred[512,1024]{1,0:T(8,128)(4,1)S(1)} %broadcast_compare_fusion.5), kind=kLoop, calls=%fused_computation.18.clone.1 | loop fusion | flops 37748736 | bytes 63488000 | tf_op jit(solution)/shard_map/while/body/eval_jaxpr/convert_element_type | solution.py:204
  450.7 11.2 %fusion.60 = f32[768,3072]{1,0:T(8,128)} fusion(bf16[1024,3072]{1,0:T(8,128)(2,1)} %get-tuple-element.384, f32[1024,768]{0,1:T(8,128)} %copy-done.9, f32[768]{0:T(1024)S(1)} %copy-done.43, f32[768]{0:T(1024)S(1)} %copy-done.34, f32[1024]{0:T(1024)S(1)} %copy-done.36, f32[1024]{0:T(1024)S(1)} %copy-done.26), kind=kOutput, calls=%fused_computation.121 | convolution fusion | flops 4835770368 | bytes 18888704 | tf_op jit(solution)/shard_map/td,tf->df/dot_general | solution.py:147
  478.3 33.6 %reduce-scatter.8.cloned.1.call-done = f32[96,2304]{1,0:T(8,128)} async-done(((f32[768,2304]{1,0:T(8,128)}), f32[96,2304]{1,0:T(8,128)}) %reduce-scatter.8.cloned.1.call-update) | async-done | bytes 884752 | tf_op jit(solution)/shard_map/reduce_scatter | solution.py:258
  539.0 18.5 %reduce-scatter.10.cloned.1.call-done = f32[96,768]{1,0:T(8,128)} async-done(((f32[768,768]{1,0:T(8,128)}), f32[96,768]{1,0:T(8,128)}) %reduce-scatter.10.cloned.1.call-update) | async-done | bytes 294928 | tf_op jit(solution)/shard_map/reduce_scatter | solution.py:260
  559.1 78.7 %reduce-scatter.12.cloned.1.call-done = f32[96,3072]{1,0:T(8,128)} async-done(((f32[768,3072]{1,0:T(8,128)}), f32[96,3072]{1,0:T(8,128)}) %reduce-scatter.12.cloned.1.call-update) | async-done | bytes 1179664 | tf_op jit(solution)/shard_map/reduce_scatter | solution.py:166
  640.0 78.2 %reduce-scatter.14.cloned.1.call-done = f32[384,768]{1,0:T(8,128)} async-done(((f32[3072,768]{1,0:T(8,128)}), f32[384,768]{1,0:T(8,128)}) %reduce-scatter.14.cloned.1.call-update) | async-done | bytes 1179664 | tf_op jit(solution)/shard_map/reduce_scatter | solution.py:168
  732.5 23.4 %all-reduce.13 = (bf16[768]{0:T(1024)(128)(2,1)S(1)}, bf16[768]{0:T(1024)(128)(2,1)S(1)}, bf16[768]{0:T(1024)(128)(2,1)S(1)}, bf16[768]{0:T(1024)(128)(2,1)S(1)}...) all-reduce(f32[768]{0:T(1024)S(1)} %get-tuple-element.293, ...), channel_id=3, replica_groups=mesh['fsdp'=8,'dp'=4] {'fsdp'}, use_global_device_ids=true, to_apply=%region_16.17.clone | all-reduce | flops 7680 | bytes 46080
  760.8 12.4 %all-reduce.15 = (bf16[96]{0:T(256)(128)(2,1)S(1)}, bf16[96]{0:T(256)(128)(2,1)S(1)}, bf16[2,96]{1,0:T(2,128)(2,1)S(1)}, bf16[96]{0:T(256)(128)(2,1)S(1)}, bf16[...) all-reduce(bf16[96]{0:T(256)(128)(2,1)S(1)} %dynamic-slice.33, ...), channel_id=1, replica_groups=mesh['fsdp'=8,'dp'=4] {'dp'}, use_global_device_ids=true, to_apply=%region_17.18 | all-reduce | flops 1152 | bytes 4608 | tf_op jit(solution)/shard_map/psum | solution.py:264
  777.4 20.2 %all-gather.17.cloned.1.call-done = bf16[384,2304]{1,0:T(8,128)(2,1)} async-done(((bf16[96,2304]{1,0:T(8,128)(2,1)}), bf16[384,2304]{1,0:T(8,128)(2,1)}) %all-gather.17.cloned.1.call-update) | async-done | bytes 1769488 | tf_op jit(solution)/shard_map/all_gather | solution.py:11
  800.4 61.2 %all-reduce.19.cloned.1.call-done = (bf16[96,768]{1,0:T(8,128)(2,1)}, bf16[96,3072]{1,0:T(8,128)(2,1)}, bf16[384,768]{1,0:T(8,128)(2,1)}) async-done(((bf16[96,768]{1,0:T(8,128)(2,1)}, bf16[96,3072]{1,0:T(8,128)(2,1)}, bf16[384,768]{1,0:T(8,128)(2,1)}), (bf16[96,768]{1,0:T(8,128)(2,1)}, bf16[96,3072]{1,0:T(8,128)(2,1)}, bf16[384,768]{1,0:T(8,128)(2,1)})) %all-reduce.19.cloned.1.call-update) | async-done | bytes 1327120 | tf_op jit(solution)/shard_map/psum | solution.py:268
  (267 shorter events, 280.8 us)
Async XLA Ops:
  7.2 61.5 %all-gather.9.cloned.1.call-start = ((), (), s32[]{:S(2)}) async-start(), calls=%async_computation.5 | async-start | bytes 3981312 | tf_op jit(solution)/shard_map/all_gather | solution.py:54
  7.9 156.1 %all-gather.11.cloned.1.call-start = ((), (), s32[]{:S(2)}) async-start(), calls=%async_computation.6 | async-start | bytes 1327104 | tf_op jit(solution)/shard_map/all_gather | solution.py:56
  8.7 161.3 %all-gather.13.cloned.1.call-start = ((), (), s32[]{:S(2)}) async-start(), calls=%async_computation.7 | async-start | bytes 5308416 | tf_op jit(solution)/shard_map/all_gather | solution.py:108
  9.4 198.4 %all-gather.15.cloned.1.call-start = ((), (), s32[]{:S(2)}) async-start(), calls=%async_computation.8 | async-start | bytes 5308416 | tf_op jit(solution)/shard_map/all_gather | solution.py:110
  10.0 501.9 %reduce-scatter.8.cloned.1.call-start = ((), (), s32[]{:S(2)}) async-start(), calls=%async_computation.9 | async-start | bytes 7962624 | tf_op jit(solution)/shard_map/reduce_scatter | solution.py:258
  44.5 24.3 %copy-start.44 = (f32[768]{0:T(1024)}, f32[768]{0:T(1024)S(1)}, u32[]{:S(2)}) copy-start(f32[768]{0:T(1024)S(1)} %convert_element_type.152) | copy-start | bytes 9220
  44.5 24.3 %copy-start.23 = (f32[768]{0:T(1024)}, f32[768]{0:T(1024)S(1)}, u32[]{:S(2)}) copy-start(f32[768]{0:T(1024)S(1)} %convert_element_type.151) | copy-start | bytes 9220
  87.7 23.5 %copy-start.4 = (bf16[1024,12,64]{0,2,1:T(8,128)(2,1)S(1)}, bf16[1024,12,64]{0,2,1:T(8,128)(2,1)}, u32[]{:S(2)}) copy-start(bf16[1024,12,64]{0,2,1:T(8,128)(2,1)} %get-tuple-element.534) | copy-start | bytes 4718596 | tf_op jit(solution)/shard_map/while
  98.7 15.8 %copy-start = (f32[12,512,1024]{2,1,0:T(8,128)S(1)}, f32[12,512,1024]{2,1,0:T(8,128)}, u32[]{:S(2)}) copy-start(f32[12,512,1024]{2,1,0:T(8,128)} %get-tuple-element.494) | copy-start | bytes 75497472 | tf_op jit(solution)/shard_map/while
  123.4 23.7 %copy-start.4 = (bf16[1024,12,64]{0,2,1:T(8,128)(2,1)S(1)}, bf16[1024,12,64]{0,2,1:T(8,128)(2,1)}, u32[]{:S(2)}) copy-start(bf16[1024,12,64]{0,2,1:T(8,128)(2,1)} %get-tuple-element.534) | copy-start | bytes 4718596 | tf_op jit(solution)/shard_map/while
  134.0 16.4 %copy-start = (f32[12,512,1024]{2,1,0:T(8,128)S(1)}, f32[12,512,1024]{2,1,0:T(8,128)}, u32[]{:S(2)}) copy-start(f32[12,512,1024]{2,1,0:T(8,128)} %get-tuple-element.494) | copy-start | bytes 75497472 | tf_op jit(solution)/shard_map/while
  168.0 77.2 %copy-start.25 = (f32[1024]{0:T(1024)}, f32[1024]{0:T(1024)S(1)}, u32[]{:S(2)}) copy-start(f32[1024]{0:T(1024)S(1)} %broadcast_multiply_fusion) | copy-start | bytes 12292
  170.0 75.1 %copy-start.35 = (f32[1024]{0:T(1024)}, f32[1024]{0:T(1024)S(1)}, u32[]{:S(2)}) copy-start(f32[1024]{0:T(1024)S(1)} %fusion.54) | copy-start | bytes 12292
  262.9 11.5 %copy-start.13 = (bf16[2,512,12,64]{1,3,2,0:T(8,128)(2,1)S(1)}, bf16[2,512,12,64]{1,3,2,0:T(8,128)(2,1)}, u32[]{:S(2)}) copy-start(bf16[2,512,12,64]{1,3,2,0:T(8,128)(2,1)} %get-tuple-element.571) | copy-start | bytes 4718596 | tf_op jit(solution)/shard_map/while
  327.1 9.5 %copy-start.3 = (bf16[2,512,12,64]{1,3,2,0:T(8,128)(2,1)S(1)}, bf16[2,512,12,64]{1,3,2,0:T(8,128)(2,1)}, u32[]{:S(2)}) copy-start(bf16[2,512,12,64]{1,3,2,0:T(8,128)(2,1)} %copy-done.2) | copy-start | bytes 4718596 | tf_op jit(solution)/shard_map/while
  346.7 11.5 %copy-start.13 = (bf16[2,512,12,64]{1,3,2,0:T(8,128)(2,1)S(1)}, bf16[2,512,12,64]{1,3,2,0:T(8,128)(2,1)}, u32[]{:S(2)}) copy-start(bf16[2,512,12,64]{1,3,2,0:T(8,128)(2,1)} %get-tuple-element.571) | copy-start | bytes 4718596 | tf_op jit(solution)/shard_map/while
  411.8 9.5 %copy-start.3 = (bf16[2,512,12,64]{1,3,2,0:T(8,128)(2,1)S(1)}, bf16[2,512,12,64]{1,3,2,0:T(8,128)(2,1)}, u32[]{:S(2)}) copy-start(bf16[2,512,12,64]{1,3,2,0:T(8,128)(2,1)} %copy-done.2) | copy-start | bytes 4718596 | tf_op jit(solution)/shard_map/while
  445.8 111.7 %reduce-scatter.10.cloned.1.call-start = ((), (), s32[]{:S(2)}) async-start(), calls=%async_computation.10 | async-start | bytes 2654208 | tf_op jit(solution)/shard_map/reduce_scatter | solution.py:260
  450.6 187.2 %reduce-scatter.12.cloned.1.call-start = ((), (), s32[]{:S(2)}) async-start(), calls=%async_computation.11 | async-start | bytes 10616832 | tf_op jit(solution)/shard_map/reduce_scatter | solution.py:166
  462.0 256.2 %reduce-scatter.14.cloned.1.call-start = ((), (), s32[]{:S(2)}) async-start(), calls=%async_computation.12 | async-start | bytes 10616832 | tf_op jit(solution)/shard_map/reduce_scatter | solution.py:168
  472.6 287.4 %reduce-scatter.16.cloned.1.call-start = ((), (), s32[]{:S(2)}) async-start(), calls=%async_computation.14 | async-start | bytes 442368
  477.0 320.6 %all-gather.17.cloned.1.call-start = ((), (), s32[]{:S(2)}) async-start(), calls=%async_computation.13 | async-start | bytes 2211840 | tf_op jit(solution)/shard_map/all_gather | solution.py:11
  513.9 347.6 %all-reduce.19.cloned.1.call-start = ((), (), s32[]{:S(2)}) async-start(), calls=%async_computation.15 | async-start | bytes 2654208 | tf_op jit(solution)/shard_map/psum | solution.py:268
  539.0 181.4 %copy-start.32 = (f32[1024]{0:T(1024)S(1)}, f32[1024]{0:T(1024)}, u32[]{:S(2)}) copy-start(f32[1024]{0:T(1024)} %copy-done.31) | copy-start | bytes 12292
  (41 other events, 151.6 us)
Sparse Core Ops, SparseCore 0:
  9.9 36.7 all-gather.8
  48.6 23.9 all-gather.10
  74.5 38.7 all-gather.12
  115.0 38.8 all-gather.14
  445.9 65.9 reduce-scatter.7
  515.1 42.3 reduce-scatter.9
  561.0 76.7 reduce-scatter.11
  641.3 76.8 reduce-scatter.13
  721.3 33.9 reduce-scatter.15
  757.3 40.2 all-gather.16
  801.3 60.1 all-reduce.18
